TPU v7x, 128 devices: a whole 4x4x4 slice. The times are simulated.
128 devices in a mesh: dom: 8 (over z, core), grp: 16 (over x, y).
Axes of the slice: x: 4, y: 4, z: 4, core: 2. Of those that a mesh axis runs over, the one named last changes fastest.
Arguments:
- src_table: float32 [16384, 400], P(('dom', 'grp')), may hold values from -8 to 8
- src_state: float32 [16384], P(('dom', 'grp')), may hold values from 0.01 to 1
- tgt_table: float32 [131072, 400], P(('dom', 'grp')), may hold values from -8 to 8
- tgt_state: float32 [131072], P(('dom', 'grp')), may hold values from 0.01 to 1
- pair_source: int32 [2, 131072], P(None, ('dom', 'grp')), may hold values from 0 to 127
- pair_owner: int32 [2, 131072, 1], P(None, ('dom', 'grp')), may hold values from 0 to 15; in each aligned block of 1024 rows (0 to 1023, 1024 to 2047, ..., all dimensions but the last counted through in order) at most 256 rows name the same one
- pair_offset: int32 [2, 131072], P(None, ('dom', 'grp')), may hold values from 0 to 1023
- negatives: int32 [8, 1000], P('dom'), may hold values from 0 to 16383
- plan: int32 [2, 8], replicated, may hold values from 0 to 7, each once within a row
Outputs:
- src_trained: float32 [16384, 400], P(('dom', 'grp'))
- src_accum: float32 [16384], P(('dom', 'grp'))
- tgt_trained: float32 [131072, 400], P(('dom', 'grp'))
- tgt_accum: float32 [131072], P(('dom', 'grp'))
Inputs may be any that keep to these rules, and one draw needn't show every extreme that they name: `pair_owner`: in every round the pairs of one device name each owner at most 256 times, and some device's pairs name some owner exactly 256 times. `plan`: each round's row names every dom index once.
All inputs are finite; a program needn't handle non-finite values.
Results may differ from a plain program's by a relative error of at most 0.011.
Values may be sent and summed in bfloat16 or wider, within the bound.
No kernel may reach another device: no remote copies, remote signals or barrier semaphores. Data moves between devices by JAX's collectives and lax.ppermute only.
A program may use at most 128 MiB of HBM per device.

v0:
```python
import jax
import jax.numpy as jnp
from jax import lax
from jax.sharding import PartitionSpec as P

LEARN = 0.1


def adagrad(emb_table, opt_state, grads):
    new_state = opt_state + jnp.mean(grads * grads, axis=1)
    return (emb_table - LEARN * grads / jnp.sqrt(new_state)[:, None], new_state)


def slot_holding(sched_row, wanted):
    return jnp.sum(
        jnp.arange(sched_row.shape[0], dtype=jnp.int32) * (sched_row == wanted).astype(jnp.int32)
    )


def relayout(emb_table, opt_state, want_slot):
    carried = (jnp.zeros_like(emb_table), jnp.zeros_like(opt_state))
    pieces = (
        lax.all_gather(emb_table, "dom", axis=0, tiled=True),
        lax.all_gather(opt_state, "dom", axis=0, tiled=True),
    )
    row_count = carried[0].shape[0]
    row_total = pieces[0].shape[0]
    local_index = jnp.arange(row_count, dtype=jnp.int32) + want_slot * row_count
    is_inside = (local_index >= 0) & (local_index < row_total)
    safe_index = jnp.clip(local_index, 0, row_total - 1)
    new_rows = jnp.where(is_inside[:, None], jnp.take(pieces[0], safe_index, axis=0), carried[0])
    new_state = jnp.where(is_inside, jnp.take(pieces[1], safe_index, axis=0), carried[1])
    return (new_rows, new_state)


def train_round(
    held_table, held_state, tgt_table, tgt_state, sources, owners, offsets, neg_ids, my_grp
):
    group_count = lax.axis_size("grp")
    src_count, emb_width = held_table.shape
    tgt_count = tgt_table.shape[0]
    pair_count = sources.shape[0]
    capacity = pair_count // 4
    slot_count = group_count * capacity
    owned_ids = neg_ids - my_grp * tgt_count
    is_mine = (owned_ids >= 0) & (owned_ids < tgt_count)
    owned_safe = jnp.clip(owned_ids, 0, tgt_count - 1)
    src_bf = held_table.astype(jnp.bfloat16)
    tgt_bf = tgt_table.astype(jnp.bfloat16)
    local_rows = jnp.where(is_mine[:, None], jnp.take(tgt_table, owned_safe, axis=0), 0.0)
    neg_rows = lax.psum(local_rows, "grp").astype(jnp.bfloat16)
    dest_onehot = (owners[:, None] == jnp.arange(group_count, dtype=jnp.int32)[None, :]).astype(
        jnp.int32
    )
    slot_rank = jnp.sum((jnp.cumsum(dest_onehot, axis=0) - 1) * dest_onehot, axis=1)
    slot_place = owners * capacity + slot_rank
    out_offsets = jnp.full((slot_count,), -1, jnp.int32).at[slot_place].set(offsets)
    outgoing = (
        jnp.zeros((slot_count, emb_width), jnp.bfloat16)
        .at[slot_place]
        .set(jnp.take(src_bf, sources, axis=0))
    )
    incoming, got_offsets = (
        lax.all_to_all(
            outgoing.reshape(group_count, capacity, emb_width),
            "grp",
            split_axis=0,
            concat_axis=0,
            tiled=True,
        ),
        lax.all_to_all(
            out_offsets.reshape(group_count, capacity),
            "grp",
            split_axis=0,
            concat_axis=0,
            tiled=True,
        ),
    )
    incoming = incoming.reshape(slot_count, emb_width)
    got_offsets = got_offsets.reshape(slot_count)
    is_valid = (got_offsets >= 0).astype(jnp.float32)
    safe_offsets = jnp.clip(got_offsets, 0, tgt_count - 1)
    target_rows = jnp.take(tgt_bf, safe_offsets, axis=0)
    positive = jnp.einsum("sd,sd->s", incoming, target_rows, preferred_element_type=jnp.float32)
    negative = lax.dot_general(
        incoming, neg_rows, (((1,), (1,)), ((), ())), preferred_element_type=jnp.float32
    )
    score_max = jnp.maximum(jnp.max(negative, axis=1), positive)
    pos_exp = jnp.exp(positive - score_max)
    neg_exp = jnp.exp(negative - score_max[:, None])
    exp_total = pos_exp + jnp.sum(neg_exp, axis=1)
    d_pos = (pos_exp / exp_total - 1.0) * is_valid
    d_neg = (neg_exp / exp_total[:, None] * is_valid[:, None]).astype(jnp.bfloat16)
    source_grad = (
        d_pos[:, None] * target_rows.astype(jnp.float32)
        + jnp.dot(d_neg, neg_rows, preferred_element_type=jnp.float32)
    ).astype(jnp.bfloat16)
    returned = lax.all_to_all(
        source_grad.reshape(group_count, capacity, emb_width),
        "grp",
        split_axis=0,
        concat_axis=0,
        tiled=True,
    ).reshape(slot_count, emb_width)
    pair_grad = jnp.take(returned, slot_place, axis=0).astype(jnp.float32)
    src_grads = jnp.zeros((src_count, emb_width), jnp.float32).at[sources].add(pair_grad)
    tgt_grads = (
        jnp.zeros((tgt_count, emb_width), jnp.float32)
        .at[safe_offsets]
        .add(d_pos[:, None] * incoming.astype(jnp.float32))
    )
    neg_part = lax.dot_general(
        d_neg, incoming, (((0,), (0,)), ((), ())), preferred_element_type=jnp.float32
    )
    summed = lax.psum(neg_part, "grp")
    tgt_grads = tgt_grads.at[owned_safe].add(jnp.where(is_mine[:, None], summed, 0.0))
    held_table, held_state = adagrad(held_table, held_state, src_grads)
    tgt_table, tgt_state = adagrad(tgt_table, tgt_state, tgt_grads)
    return (held_table, held_state, tgt_table, tgt_state)


def shards(
    src_table,
    src_state,
    tgt_table,
    tgt_state,
    pair_source,
    pair_owner,
    pair_offset,
    negatives,
    plan,
):
    my_dom = lax.axis_index("dom")
    my_grp = lax.axis_index("grp")
    round_count = plan.shape[0]
    neg_ids = negatives[0]
    for round_index in range(round_count):
        held_table, held_state = relayout(src_table, src_state, plan[round_index, my_dom])
        held_table, held_state, tgt_table, tgt_state = train_round(
            held_table,
            held_state,
            tgt_table,
            tgt_state,
            pair_source[round_index],
            pair_owner[round_index, :, 0],
            pair_offset[round_index],
            neg_ids,
            my_grp,
        )
        src_table, src_state = relayout(
            held_table, held_state, slot_holding(plan[round_index], my_dom)
        )
    return (src_table, src_state, tgt_table, tgt_state)


def solution(mesh):
    return jax.shard_map(
        shards,
        mesh=mesh,
        in_specs=(
            P(("dom", "grp"), None),
            P(("dom", "grp")),
            P(("dom", "grp"), None),
            P(("dom", "grp")),
            P(None, ("dom", "grp")),
            P(None, ("dom", "grp"), None),
            P(None, ("dom", "grp")),
            P("dom", None),
            P(),
        ),
        out_specs=(
            P(("dom", "grp"), None),
            P(("dom", "grp")),
            P(("dom", "grp"), None),
            P(("dom", "grp")),
        ),
        check_vma=False,
    )
```

profile of v0, /device:TPU:1, one launch (start us, length us, event | category | flops | bytes accessed | tf_op | source)
XLA Modules:
  0.0 816.0 jit_solution(2772978685348490794)
XLA Ops:
  42.0 13.0 %scatter_custom_fusion.1 = bf16[4096,400]{1,0:T(8,128)(2,1)} fusion(s32[1024]{0:T(1024)S(1)} %bitcast.168, bf16[]{:T(256)} %constant.84.clone.1, pred[1024]{0:T(1024)(128)(4,1)S(1)} %compare_and_fusion.6, bf16[]{:T(256)} %constant.29.clone.2, bf16[128,400]{1,0:T(8,128)(2,1)S(1)} %fusion.38, s32[1024]{0:T(1024)S(1)} %fusion.56), kind=kCustom, calls=%fused_computation.58 | custom fusion | flops 409600 | bytes 3412996 | tf_op jit(solution)/shard_map/scatter | solution.py:61
  83.4 97.5 %all-reduce.8 = bf16[1000,400]{0,1:T(8,128)(2,1)} all-reduce(f32[1000,400]{0,1:T(8,128)S(1)} %select_select_fusion.1), channel_id=1, replica_groups=mesh['dom'=8,'grp'=16] {'grp'}, use_global_device_ids=true, to_apply=%region_7.12 | all-reduce | flops 400000 | bytes 2400000 | tf_op jit(solution)/shard_map/psum | solution.py:51
  181.1 17.3 %gather_fusion.1 = bf16[4096,400]{1,0:T(8,128)(2,1)} fusion(bf16[1024,400]{1,0:T(8,128)(2,1)S(1)} %copy.82, s32[4096]{0:T(1024)S(1)} %fusion.48), kind=kCustom, calls=%fused_computation.2.clone | custom fusion | bytes 6569984 | tf_op jit(solution)/shard_map/jit(_take)/gather | solution.py:83
  206.9 8.0 fusion.77
  242.8 21.5 %all-gather = f32[8,1,128]{2,1,0:T(1,128)S(1)} all-gather(f32[1,1,128]{2,1,0:T(1,128)S(1)} %bitcast.173), channel_id=1, replica_groups=mesh['dom'=8,'grp'=16] {'dom'}, dimensions={0}, use_global_device_ids=true | all-gather | bytes 4608 | tf_op jit(solution)/shard_map/all_gather | solution.py:24
  276.0 15.2 %scatter_custom_fusion.2 = f32[128,400]{1,0:T(8,128)} fusion(s32[1024]{0:T(1024)} %bitcast.169, pred[1024]{0:T(1024)(128)(4,1)} %compare_and_fusion.4, bf16[]{:T(256)} %constant.29.clone.2, f32[]{:T(128)} %constant.60.clone.1, bf16[4096,400]{1,0:T(8,128)(2,1)} %bitcast.126, s32[1024]{0:T(1024)} %broadcast_clamp_fusion.3), kind=kCustom, calls=%fused_computation.54 | custom fusion | flops 1228800 | bytes 4405248 | tf_op jit(solution)/shard_map/scatter-add | solution.py:106
  300.1 16.7 %all-to-all-start.3 = ((s32[16,1,256]{2,1,0:T(1,128)}), s32[16,1,256]{2,1,0:T(1,128)}, u32[]{:S(2)}, u32[]{:S(2)}) async-start(s32[16,1,256]{2,1,0:T(1,128)} %bitcast.32), calls=%async_computation.3 | async-start | bytes 32768 | tf_op jit(solution)/shard_map/all_to_all | solution.py:71
  324.4 11.6 %all-gather.11.cloned.1.call-done = f32[1024,400]{1,0:T(8,128)} async-done(((f32[128,400]{1,0:T(8,128)}), f32[1024,400]{1,0:T(8,128)}) %all-gather.11.cloned.1.call-update) | async-done | bytes 1638416 | tf_op jit(solution)/shard_map/all_gather | solution.py:23
  352.4 13.7 %all-gather.13.cloned.1.call-done = f32[1024,400]{1,0:T(8,128)} async-done(((f32[128,400]{1,0:T(8,128)}), f32[1024,400]{1,0:T(8,128)}) %all-gather.13.cloned.1.call-update) | async-done | bytes 1638416 | tf_op jit(solution)/shard_map/all_gather | solution.py:23
  370.1 15.9 %scatter_custom_fusion.4 = bf16[4096,400]{1,0:T(8,128)(2,1)} fusion(s32[1024]{0:T(1024)} %bitcast.164, bf16[]{:T(256)} %constant.84.clone.1, pred[1024]{0:T(1024)(128)(4,1)S(1)} %copy-done.40, bf16[]{:T(256)} %constant.29.clone.2, bf16[128,400]{1,0:T(8,128)(2,1)} %fusion.39, s32[1024]{0:T(1024)S(1)} %copy-done.32), kind=kCustom, calls=%fused_computation.56 | custom fusion | flops 409600 | bytes 3414016 | tf_op jit(solution)/shard_map/scatter | solution.py:61
  403.2 8.5 %copy.92 = f32[4096,400]{1,0:T(8,128)} copy(f32[4096,400]{0,1:T(8,128)} %convert_multiply_fusion.2) | data formatting | bytes 13107200 | tf_op jit(solution)/shard_map/mul | solution.py:110
  411.7 29.3 %scatter_custom_fusion.5 = f32[1024,400]{1,0:T(8,128)S(1)} fusion(s32[4096]{0:T(1024)} %bitcast.161, f32[4096,400]{1,0:T(8,128)} %copy.92, f32[]{:T(128)} %constant.60.clone.1), kind=kCustom, calls=%fused_computation.68 | custom fusion | flops 1638400 | bytes 1638912 | tf_op jit(solution)/shard_map/scatter-add | solution.py:110
  441.0 48.3 %all-reduce.5.cloned.1.call-done = f32[1000,400]{0,1:T(8,128)} async-done(((f32[1000,400]{0,1:T(8,128)}), f32[1000,400]{0,1:T(8,128)}) %all-reduce.5.cloned.1.call-update) | async-done | bytes 1600016 | tf_op jit(solution)/shard_map/psum | solution.py:115
  495.0 8.7 %scatter_fusion = f32[1024,400]{1,0:T(8,128)S(1)} fusion(f32[1024,400]{1,0:T(8,128)S(1)} %scatter_custom_fusion.5, s32[1000]{0:T(1024)S(1)} %bitcast.151, f32[1000,400]{1,0:T(8,128)} %copy.93), kind=kCustom, calls=%fused_computation.22 | custom fusion | flops 400000 | bytes 4804000 | tf_op jit(solution)/shard_map/scatter-add | solution.py:116
  516.2 17.3 %gather_fusion.6 = bf16[4096,400]{1,0:T(8,128)(2,1)} fusion(bf16[1024,400]{1,0:T(8,128)(2,1)S(1)} %get-tuple-element.32, s32[4096]{0:T(1024)S(1)} %copy-done.16), kind=kCustom, calls=%fused_computation.10.clone | custom fusion | bytes 6569984 | tf_op jit(solution)/shard_map/jit(_take)/gather | solution.py:83
  539.5 73.8 %all-reduce.9 = bf16[1000,400]{0,1:T(8,128)(2,1)} all-reduce(f32[1000,400]{0,1:T(8,128)S(1)} %select_select_fusion), channel_id=1, replica_groups=mesh['dom'=8,'grp'=16] {'grp'}, use_global_device_ids=true, to_apply=%region_21.28 | all-reduce | flops 400000 | bytes 2400000 | tf_op jit(solution)/shard_map/psum | solution.py:51
  615.7 8.0 fusion.78
  661.8 28.2 %all-gather.1 = f32[8,1,128]{2,1,0:T(1,128)S(1)} all-gather(f32[1,1,128]{2,1,0:T(1,128)} %bitcast.171), channel_id=1, replica_groups=mesh['dom'=8,'grp'=16] {'dom'}, dimensions={0}, use_global_device_ids=true | all-gather | bytes 4608 | tf_op jit(solution)/shard_map/all_gather | solution.py:24
  692.3 8.5 %all-gather.2 = f32[8,1,128]{2,1,0:T(1,128)S(1)} all-gather(f32[1,1,128]{2,1,0:T(1,128)S(1)} %fusion.62), channel_id=1, replica_groups=mesh['dom'=8,'grp'=16] {'dom'}, dimensions={0}, use_global_device_ids=true | all-gather | bytes 4608 | tf_op jit(solution)/shard_map/all_gather | solution.py:24
  708.4 15.0 %scatter_custom_fusion.7 = f32[128,400]{1,0:T(8,128)} fusion(s32[1024]{0:T(1024)} %bitcast.165, pred[1024]{0:T(1024)(128)(4,1)S(1)} %copy-done.41, bf16[]{:T(256)} %constant.29.clone.2, f32[]{:T(128)} %constant.60.clone.1, bf16[4096,400]{1,0:T(8,128)(2,1)} %bitcast.125, s32[1024]{0:T(1024)S(1)} %copy-done.31), kind=kCustom, calls=%fused_computation.50 | custom fusion | flops 1228800 | bytes 4405248 | tf_op jit(solution)/shard_map/scatter-add | solution.py:106
  732.1 8.6 %copy.99 = f32[4096,400]{1,0:T(8,128)} copy(f32[4096,400]{0,1:T(8,128)} %convert_multiply_fusion) | data formatting | bytes 13107200 | tf_op jit(solution)/shard_map/mul | solution.py:110
  740.6 29.4 %scatter_custom_fusion.8 = f32[1024,400]{1,0:T(8,128)S(1)} fusion(s32[4096]{0:T(1024)S(1)} %bitcast.162, f32[4096,400]{1,0:T(8,128)} %copy.99, f32[]{:T(128)} %constant.60.clone.1), kind=kCustom, calls=%fused_computation.66 | custom fusion | flops 1638400 | bytes 1638912 | tf_op jit(solution)/shard_map/scatter-add | solution.py:110
  776.1 8.8 %scatter_fusion.1 = f32[1024,400]{1,0:T(8,128)S(1)} fusion(f32[1024,400]{1,0:T(8,128)S(1)} %scatter_custom_fusion.8, s32[1000]{0:T(1024)S(1)} %bitcast.152, f32[1000,400]{1,0:T(8,128)} %copy.100), kind=kCustom, calls=%fused_computation.25 | custom fusion | flops 400000 | bytes 4804000 | tf_op jit(solution)/shard_map/scatter-add | solution.py:116
  791.1 12.7 %all-gather.3 = f32[8,1,128]{2,1,0:T(1,128)S(1)} all-gather(f32[1,1,128]{2,1,0:T(1,128)S(1)} %bitcast.172), channel_id=1, replica_groups=mesh['dom'=8,'grp'=16] {'dom'}, dimensions={0}, use_global_device_ids=true | all-gather | bytes 4608 | tf_op jit(solution)/shard_map/all_gather | solution.py:24
  (256 shorter events, 262.7 us)
Async XLA Ops:
  7.2 32.2 %all-gather.9.cloned.1.call-start = ((), (), s32[]{:S(2)}) async-start(), calls=%async_computation.6 | async-start | bytes 2359296 | tf_op jit(solution)/shard_map/all_gather | solution.py:23
  9.7 28.6 %copy-start.14 = (s32[1,1024,1]{1,2,0:T(1,128)}, s32[1,1024,1]{1,2,0:T(1,128)S(1)}, u32[]{:S(2)}) copy-start(s32[1,1024,1]{1,2,0:T(1,128)S(1)} %get-tuple-element.49) | copy-start | bytes 12292
  19.5 18.8 %copy-start.19 = (s32[1024]{0:T(1024)}, s32[1024]{0:T(1024)S(1)}, u32[]{:S(2)}) copy-start(s32[1024]{0:T(1024)S(1)} %fusion.43) | copy-start | bytes 12292
  27.2 33.8 %all-to-all-start = ((s32[16,1,256]{2,1,0:T(1,128)}), s32[16,1,256]{2,1,0:T(1,128)S(1)}, u32[]{:S(2)}, u32[]{:S(2)}) async-start(s32[16,1,256]{2,1,0:T(1,128)} %bitcast.14), calls=%async_computation | async-start | bytes 32768 | tf_op jit(solution)/shard_map/all_to_all | solution.py:71
  36.9 18.1 %copy-start.43 = (pred[128]{0:T(512)(128)(4,1)}, pred[128]{0:T(512)(128)(4,1)S(1)}, u32[]{:S(2)}) copy-start(pred[128]{0:T(512)(128)(4,1)S(1)} %get-tuple-element.58) | copy-start | bytes 388
  41.8 19.2 %copy-start.9 = (f32[128,400]{1,0:T(8,128)}, f32[128,400]{1,0:T(8,128)S(1)}, u32[]{:S(2)}) copy-start(f32[128,400]{1,0:T(8,128)S(1)} %gather_fusion) | copy-start | bytes 614404
  61.1 143.3 %all-to-all-start.1 = ((bf16[16,256,400]{1,2,0:T(8,128)(2,1)}), bf16[16,256,400]{1,2,0:T(8,128)(2,1)}, u32[]{:S(2)}, u32[]{:S(2)}) async-start(bf16[16,256,400]{1,2,0:T(8,128)(2,1)} %copy.80), calls=%async_computation.1 | async-start | bytes 6553600 | tf_op jit(solution)/shard_map/all_to_all | solution.py:64
  238.1 28.9 %copy-start.27 = (s32[2,1024]{1,0:T(2,128)S(1)}, s32[2,1024]{1,0:T(2,128)}, u32[]{:S(2)}) copy-start(s32[2,1024]{1,0:T(2,128)} %param.25) | copy-start | bytes 24580
  238.1 31.9 %all-to-all-start.2 = ((bf16[16,256,400]{1,2,0:T(8,128)(2,1)}), bf16[16,256,400]{1,2,0:T(8,128)(2,1)}, u32[]{:S(2)}, u32[]{:S(2)}) async-start(bf16[16,256,400]{1,2,0:T(8,128)(2,1)} %bitcast.130), calls=%async_computation.2 | async-start | bytes 6553600 | tf_op jit(solution)/shard_map/all_to_all | solution.py:98
  242.7 93.3 %all-gather.11.cloned.1.call-start = ((), (), s32[]{:S(2)}) async-start(), calls=%async_computation.7 | async-start | bytes 2359296 | tf_op jit(solution)/shard_map/all_gather | solution.py:23
  300.1 40.5 %all-to-all-start.3 = ((s32[16,1,256]{2,1,0:T(1,128)}), s32[16,1,256]{2,1,0:T(1,128)}, u32[]{:S(2)}, u32[]{:S(2)}) async-start(s32[16,1,256]{2,1,0:T(1,128)} %bitcast.32), calls=%async_computation.3 | async-start | bytes 32768 | tf_op jit(solution)/shard_map/all_to_all | solution.py:71
  316.8 49.3 %all-gather.13.cloned.1.call-start = ((), (), s32[]{:S(2)}) async-start(), calls=%async_computation.8 | async-start | bytes 2359296 | tf_op jit(solution)/shard_map/all_gather | solution.py:23
  340.1 149.2 %all-reduce.5.cloned.1.call-start = ((), (), s32[]{:S(2)}) async-start(), calls=%async_computation.9 | async-start | bytes 3276800 | tf_op jit(solution)/shard_map/psum | solution.py:115
  351.7 18.3 %copy-start.32 = (s32[1024]{0:T(1024)S(1)}, s32[1024]{0:T(1024)}, u32[]{:S(2)}) copy-start(s32[1024]{0:T(1024)} %fusion.57) | copy-start | bytes 12292
  351.7 18.3 %copy-start.40 = (pred[1024]{0:T(1024)(128)(4,1)S(1)}, pred[1024]{0:T(1024)(128)(4,1)}, u32[]{:S(2)}) copy-start(pred[1024]{0:T(1024)(128)(4,1)} %compare_and_fusion.3) | copy-start | bytes 3076
  392.0 221.3 %all-to-all-start.4 = ((bf16[16,256,400]{1,2,0:T(8,128)(2,1)}), bf16[16,256,400]{1,2,0:T(8,128)(2,1)}, u32[]{:S(2)}, u32[]{:S(2)}) async-start(bf16[16,256,400]{1,2,0:T(8,128)(2,1)} %copy.90), calls=%async_computation.4 | async-start | bytes 6553600 | tf_op jit(solution)/shard_map/all_to_all | solution.py:64
  403.2 86.2 %copy-start.29 = (pred[1000]{0:T(1024)(128)(4,1)S(1)}, pred[1000]{0:T(1024)(128)(4,1)}, u32[]{:S(2)}) copy-start(pred[1000]{0:T(1024)(128)(4,1)} %copy-done.28) | copy-start | bytes 3004
  441.0 54.0 %copy-start.22 = (s32[1000,1]{0,1:T(1,128)S(1)}, s32[1000,1]{0,1:T(1,128)}, u32[]{:S(2)}) copy-start(s32[1000,1]{0,1:T(1,128)} %get-tuple-element.34) | copy-start | bytes 12004
  646.9 55.5 %all-to-all-start.5 = ((bf16[16,256,400]{1,2,0:T(8,128)(2,1)}), bf16[16,256,400]{1,2,0:T(8,128)(2,1)}, u32[]{:S(2)}, u32[]{:S(2)}) async-start(bf16[16,256,400]{1,2,0:T(8,128)(2,1)} %bitcast.129), calls=%async_computation.5 | async-start | bytes 6553600 | tf_op jit(solution)/shard_map/all_to_all | solution.py:98
  651.4 119.0 %all-reduce.7.cloned.1.call-start = ((), (), s32[]{:S(2)}) async-start(), calls=%async_computation.11 | async-start | bytes 3276800 | tf_op jit(solution)/shard_map/psum | solution.py:115
  659.4 146.1 %all-gather.15.cloned.1.call-start = ((), (), s32[]{:S(2)}) async-start(), calls=%async_computation.10 | async-start | bytes 2359296 | tf_op jit(solution)/shard_map/all_gather | solution.py:23
  732.1 38.4 %copy-start.30 = (pred[1000]{0:T(1024)(128)(4,1)S(1)}, pred[1000]{0:T(1024)(128)(4,1)}, u32[]{:S(2)}) copy-start(pred[1000]{0:T(1024)(128)(4,1)} %copy-done.28) | copy-start | bytes 3004
  788.3 19.7 %copy-start.46 = (pred[128]{0:T(512)(128)(4,1)S(1)}, pred[128]{0:T(512)(128)(4,1)}, u32[]{:S(2)}) copy-start(pred[128]{0:T(512)(128)(4,1)} %get-tuple-element.64) | copy-start | bytes 388
  788.3 19.7 %copy-start.47 = (pred[128]{0:T(512)(128)(4,1)S(1)}, pred[128]{0:T(512)(128)(4,1)}, u32[]{:S(2)}) copy-start(pred[128]{0:T(512)(128)(4,1)} %get-tuple-element.65) | copy-start | bytes 388
  (36 other events, 230.2 us)
Sparse Core Ops, SparseCore 0:
  10.3 29.0 all-gather.8
  295.2 40.8 all-gather.10
  340.3 25.7 all-gather.12
  369.8 119.4 all-reduce.4
  659.5 110.9 all-reduce.6
  772.0 26.9 all-gather.14
where the time goes:
time: 828 us; the launch traced here: 816 us
  blocking collectives  242 us (29%)
  other arithmetic  231 us (28%)
  local copies, waits for them, and re-layouts  160 us (19%)
  waiting for transfers between devices  77.6 us (9%)
  starting transfers between devices  47.5 us (6%)
  matrix products  39.2 us (5%)
  between operations  17.8 us (2%)
    psum x2, blocking collectives, train_round(): neg_rows = lax.psum(local_rows, 'grp').astype(jnp.bfloat16)  171 us
    all_gather x4, blocking collectives, relayout(): lax.all_gather(opt_state, 'dom', axis=0, tiled=True)  71 us
    scatter-add x2, other arithmetic, train_round(): tgt_grads = jnp.zeros((tgt_count, emb_width), jnp.float32).at[safe_offset...  58.7 us
    psum x2, waiting for transfers between devices, train_round(): summed = lax.psum(neg_part, 'grp')  48.7 us
    gather x4, local copies, waits for them, and re-layouts, train_round(): target_rows = jnp.take(tgt_bf, safe_offsets, axis=0)  46.6 us
    scatter-add x2, other arithmetic, train_round(): jnp.zeros((src_count, emb_width), jnp.float32).at[sources].add(pair_grad)  30.2 us
    scatter x2, other arithmetic, train_round(): outgoing = jnp.zeros((slot_count, emb_width), jnp.bfloat16).at[slot_place...  28.9 us
    all_gather x4, waiting for transfers between devices, relayout(): lax.all_gather(emb_table, 'dom', axis=0, tiled=True)  26.4 us
  transfers between devices with their start and end apart: 12, of which 6 were waited for; matrix products, arithmetic and copies ran while one was open for 40% of the time, Pallas kernels for 0%

commit v1 on v0

--- a/solution.py
+++ b/solution.py
@@ -112,7 +112,9 @@
     neg_part = lax.dot_general(
         d_neg, incoming, (((0,), (0,)), ((), ())), preferred_element_type=jnp.float32
     )
-    summed = lax.psum(neg_part, "grp")
+    summed = neg_part
+    for hop in (1, 2, 4, 8):
+        summed = summed + lax.ppermute(summed, "grp", [(dev, dev ^ hop) for dev in range(16)])
     tgt_grads = tgt_grads.at[owned_safe].add(jnp.where(is_mine[:, None], summed, 0.0))
     held_table, held_state = adagrad(held_table, held_state, src_grads)
     tgt_table, tgt_state = adagrad(tgt_table, tgt_state, tgt_grads)

time: 828 us -> 937 us (1.13)
  waiting for transfers between devices: 77.6 us -> 140 us
  starting transfers between devices: 47.5 us -> 92.9 us
  other arithmetic: 231 us -> 242 us
    ppermute x0 -> x8, waiting for transfers between devices: none -> 135 us  [train_round(): lax.ppermute(summed, 'grp', [(dev, dev ^ hop) for dev in range(16)])]
    psum x2 -> x0, waiting for transfers between devices: 48.7 us -> none  [train_round(): summed = lax.psum(neg_part, 'grp')]
    ppermute x0 -> x8, starting transfers between devices: none -> 45.9 us  [train_round(): lax.ppermute(summed, 'grp', [(dev, dev ^ hop) for dev in range(16)])]
    all_gather x4, waiting for transfers between devices: 26.4 us -> 1.1 us  [relayout(): lax.all_gather(emb_table, 'dom', axis=0, tiled=True)]
    add x0 -> x6, other arithmetic: none -> 16.8 us  [train_round(): summed + lax.ppermute(summed, 'grp', [(dev, dev ^ hop) for dev in range(1...]
    all_gather x4, blocking collectives: 71 us -> 59.1 us  [relayout(): lax.all_gather(opt_state, 'dom', axis=0, tiled=True)]
  transfers between devices with their start and end apart: 12 -> 18, of which waited for: 6 -> 6; matrix products, arithmetic and copies ran while one was open for 40% -> 34% of each run, Pallas kernels for 0% -> 0%
where the time goes in v1:
time: 937 us; the launch traced here: 925 us
  other arithmetic  242 us (26%)
  blocking collectives  237 us (25%)
  local copies, waits for them, and re-layouts  160 us (17%)
  waiting for transfers between devices  140 us (15%)
  starting transfers between devices  92.9 us (10%)
  matrix products  36.8 us (4%)
  between operations  17.4 us (2%)
    psum x2, blocking collectives, train_round(): neg_rows = lax.psum(local_rows, 'grp').astype(jnp.bfloat16)  177 us
    ppermute x8, waiting for transfers between devices, train_round(): lax.ppermute(summed, 'grp', [(dev, dev ^ hop) for dev in range(16)])  135 us
    all_gather x4, blocking collectives, relayout(): lax.all_gather(opt_state, 'dom', axis=0, tiled=True)  59.1 us
    scatter-add x2, other arithmetic, train_round(): tgt_grads = jnp.zeros((tgt_count, emb_width), jnp.float32).at[safe_offset...  58.7 us
    gather x4, local copies, waits for them, and re-layouts, train_round(): target_rows = jnp.take(tgt_bf, safe_offsets, axis=0)  46.9 us
    ppermute x8, starting transfers between devices, train_round(): lax.ppermute(summed, 'grp', [(dev, dev ^ hop) for dev in range(16)])  45.9 us
    scatter-add x2, other arithmetic, train_round(): jnp.zeros((src_count, emb_width), jnp.float32).at[sources].add(pair_grad)  29.9 us
    scatter x2, other arithmetic, train_round(): outgoing = jnp.zeros((slot_count, emb_width), jnp.bfloat16).at[slot_place...  28.7 us
  transfers between devices with their start and end apart: 18, of which 6 were waited for; matrix products, arithmetic and copies ran while one was open for 34% of the time, Pallas kernels for 0%

profile of v1, /device:TPU:1, one launch (start us, length us, event | category | flops | bytes accessed | tf_op | source)
XLA Modules:
  0.0 925.2 jit_solution(16210407582164569114)
XLA Ops:
  41.9 13.0 %scatter_custom_fusion.1 = bf16[4096,400]{1,0:T(8,128)(2,1)} fusion(s32[1024]{0:T(1024)S(1)} %bitcast.168, bf16[]{:T(256)} %constant.84.clone.1, pred[1024]{0:T(1024)(128)(4,1)S(1)} %compare_and_fusion.6, bf16[]{:T(256)} %constant.29.clone.2, bf16[128,400]{1,0:T(8,128)(2,1)S(1)} %fusion.38, s32[1024]{0:T(1024)S(1)} %fusion.56), kind=kCustom, calls=%fused_computation.58 | custom fusion | flops 409600 | bytes 3412996 | tf_op jit(solution)/shard_map/scatter | solution.py:61
  82.7 98.5 %all-reduce.2 = bf16[1000,400]{0,1:T(8,128)(2,1)} all-reduce(f32[1000,400]{0,1:T(8,128)S(1)} %select_select_fusion.1), channel_id=1, replica_groups=mesh['dom'=8,'grp'=16] {'grp'}, use_global_device_ids=true, to_apply=%region_7.12 | all-reduce | flops 400000 | bytes 2400000 | tf_op jit(solution)/shard_map/psum | solution.py:51
  181.3 17.3 %gather_fusion.1 = bf16[4096,400]{1,0:T(8,128)(2,1)} fusion(bf16[1024,400]{1,0:T(8,128)(2,1)S(1)} %copy.82, s32[4096]{0:T(1024)S(1)} %fusion.48), kind=kCustom, calls=%fused_computation.2.clone | custom fusion | bytes 6569984 | tf_op jit(solution)/shard_map/jit(_take)/gather | solution.py:83
  243.8 21.3 %all-gather = f32[8,1,128]{2,1,0:T(1,128)S(1)} all-gather(f32[1,1,128]{2,1,0:T(1,128)S(1)} %bitcast.173), channel_id=1, replica_groups=mesh['dom'=8,'grp'=16] {'dom'}, dimensions={0}, use_global_device_ids=true | all-gather | bytes 4608 | tf_op jit(solution)/shard_map/all_gather | solution.py:24
  277.2 14.9 %scatter_custom_fusion.2 = f32[128,400]{1,0:T(8,128)} fusion(s32[1024]{0:T(1024)S(1)} %bitcast.169, pred[1024]{0:T(1024)(128)(4,1)S(1)} %compare_and_fusion.4, bf16[]{:T(256)} %constant.29.clone.2, f32[]{:T(128)} %constant.60.clone.1, bf16[4096,400]{1,0:T(8,128)(2,1)} %bitcast.126, s32[1024]{0:T(1024)S(1)} %broadcast_clamp_fusion.3), kind=kCustom, calls=%fused_computation.54 | custom fusion | flops 1228800 | bytes 3486726 | tf_op jit(solution)/shard_map/scatter-add | solution.py:106
  303.9 21.0 %collective-permute-done = f32[1000,400]{0,1:T(8,128)S(1)} collective-permute-done((f32[1000,400]{0,1:T(8,128)S(1)}, f32[1000,400]{0,1:T(8,128)S(1)}, u32[]{:S(2)}, u32[]{:S(2)}) %collective-permute-start) | collective-permute-done | bytes 1600032 | tf_op jit(solution)/shard_map/ppermute | solution.py:117
  326.3 9.0 collective-permute-start.1
  346.8 18.8 %all-to-all-start.3 = ((s32[16,1,256]{2,1,0:T(1,128)}), s32[16,1,256]{2,1,0:T(1,128)S(1)}, u32[]{:S(2)}, u32[]{:S(2)}) async-start(s32[16,1,256]{2,1,0:T(1,128)} %bitcast.32), calls=%async_computation.3 | async-start | bytes 32768 | tf_op jit(solution)/shard_map/all_to_all | solution.py:71
  376.7 20.7 %collective-permute-done.2 = f32[1000,400]{0,1:T(8,128)} collective-permute-done((f32[1000,400]{0,1:T(8,128)}, f32[1000,400]{0,1:T(8,128)}, u32[]{:S(2)}, u32[]{:S(2)}) %collective-permute-start.2) | collective-permute-done | bytes 1600032 | tf_op jit(solution)/shard_map/ppermute | solution.py:117
  400.8 25.1 %collective-permute-start.3 = (f32[1000,400]{0,1:T(8,128)}, f32[1000,400]{0,1:T(8,128)}, u32[]{:S(2)}, u32[]{:S(2)}) collective-permute-start(f32[1000,400]{0,1:T(8,128)} %add.272), channel_id=1, source_target_pairs={{0,8},{1,9},{2,10},{3,11},{4,12},{5,13},{6,14},{7,15},{8,0},{9,1},... | collective-permute-start | bytes 4800008 | tf_op jit(solution)/shard_map/ppermute | solution.py:117
  430.0 15.6 %scatter_custom_fusion.4 = bf16[4096,400]{1,0:T(8,128)(2,1)} fusion(s32[1024]{0:T(1024)} %bitcast.164, bf16[]{:T(256)} %constant.84.clone.1, pred[1024]{0:T(1024)(128)(4,1)S(1)} %copy-done.43, bf16[]{:T(256)} %constant.29.clone.2, bf16[128,400]{1,0:T(8,128)(2,1)} %fusion.39, s32[1024]{0:T(1024)S(1)} %copy-done.34), kind=kCustom, calls=%fused_computation.56 | custom fusion | flops 409600 | bytes 3414016 | tf_op jit(solution)/shard_map/scatter | solution.py:61
  469.2 29.3 %scatter_custom_fusion.5 = f32[1024,400]{1,0:T(8,128)S(1)} fusion(s32[4096]{0:T(1024)} %bitcast.161, f32[4096,400]{1,0:T(8,128)} %copy.92, f32[]{:T(128)} %constant.60.clone.1), kind=kCustom, calls=%fused_computation.70 | custom fusion | flops 1638400 | bytes 1638912 | tf_op jit(solution)/shard_map/scatter-add | solution.py:110
  504.9 8.7 scatter_fusion
  517.0 17.3 %gather_fusion.6 = bf16[4096,400]{1,0:T(8,128)(2,1)} fusion(bf16[1024,400]{1,0:T(8,128)(2,1)S(1)} %get-tuple-element.32, s32[4096]{0:T(1024)S(1)} %copy-done.19), kind=kCustom, calls=%fused_computation.10.clone | custom fusion | bytes 6569984 | tf_op jit(solution)/shard_map/jit(_take)/gather | solution.py:83
  547.8 78.9 %all-reduce.3 = bf16[1000,400]{0,1:T(8,128)(2,1)} all-reduce(f32[1000,400]{0,1:T(8,128)S(1)} %select_select_fusion), channel_id=1, replica_groups=mesh['dom'=8,'grp'=16] {'grp'}, use_global_device_ids=true, to_apply=%region_20.27 | all-reduce | flops 400000 | bytes 2400000 | tf_op jit(solution)/shard_map/psum | solution.py:51
  672.6 58.3 %collective-permute-done.4 = f32[1000,400]{0,1:T(8,128)S(1)} collective-permute-done((f32[1000,400]{0,1:T(8,128)S(1)}, f32[1000,400]{0,1:T(8,128)S(1)}, u32[]{:S(2)}, u32[]{:S(2)}) %collective-permute-start.4) | collective-permute-done | bytes 1600032 | tf_op jit(solution)/shard_map/ppermute | solution.py:117
  734.7 19.0 %all-gather.1 = f32[8,1,128]{2,1,0:T(1,128)S(1)} all-gather(f32[1,1,128]{2,1,0:T(1,128)S(1)} %bitcast.171), channel_id=1, replica_groups=mesh['dom'=8,'grp'=16] {'dom'}, dimensions={0}, use_global_device_ids=true | all-gather | bytes 4608 | tf_op jit(solution)/shard_map/all_gather | solution.py:24
  756.1 9.8 %all-gather.2 = f32[8,1,128]{2,1,0:T(1,128)S(1)} all-gather(f32[1,1,128]{2,1,0:T(1,128)S(1)} %fusion.62), channel_id=1, replica_groups=mesh['dom'=8,'grp'=16] {'dom'}, dimensions={0}, use_global_device_ids=true | all-gather | bytes 4608 | tf_op jit(solution)/shard_map/all_gather | solution.py:24
  773.5 15.0 %scatter_custom_fusion.7 = f32[128,400]{1,0:T(8,128)} fusion(s32[1024]{0:T(1024)} %bitcast.165, pred[1024]{0:T(1024)(128)(4,1)} %compare_and_fusion.2, bf16[]{:T(256)} %constant.29.clone.2, f32[]{:T(128)} %constant.60.clone.1, bf16[4096,400]{1,0:T(8,128)(2,1)} %bitcast.125, s32[1024]{0:T(1024)S(1)} %copy-done.33), kind=kCustom, calls=%fused_computation.50 | custom fusion | flops 1228800 | bytes 4405248 | tf_op jit(solution)/shard_map/scatter-add | solution.py:106
  796.5 35.3 %collective-permute-done.6 = f32[1000,400]{0,1:T(8,128)} collective-permute-done((f32[1000,400]{0,1:T(8,128)}, f32[1000,400]{0,1:T(8,128)}, u32[]{:S(2)}, u32[]{:S(2)}) %collective-permute-start.6) | collective-permute-done | bytes 1600032 | tf_op jit(solution)/shard_map/ppermute | solution.py:117
  845.5 8.5 copy.99
  854.1 29.4 %scatter_custom_fusion.8 = f32[1024,400]{1,0:T(8,128)S(1)} fusion(s32[4096]{0:T(1024)S(1)} %bitcast.162, f32[4096,400]{1,0:T(8,128)} %copy.99, f32[]{:T(128)} %constant.60.clone.1), kind=kCustom, calls=%fused_computation.68 | custom fusion | flops 1638400 | bytes 1638912 | tf_op jit(solution)/shard_map/scatter-add | solution.py:110
  883.5 9.0 all-gather.3
  903.7 8.7 scatter_fusion.1
  (286 shorter events, 305.2 us)
Async XLA Ops:
  7.2 32.2 %all-gather.9.cloned.1.call-start = ((), (), s32[]{:S(2)}) async-start(), calls=%async_computation.6 | async-start | bytes 2359296 | tf_op jit(solution)/shard_map/all_gather | solution.py:23
  27.2 33.9 %all-to-all-start = ((s32[16,1,256]{2,1,0:T(1,128)}), s32[16,1,256]{2,1,0:T(1,128)S(1)}, u32[]{:S(2)}, u32[]{:S(2)}) async-start(s32[16,1,256]{2,1,0:T(1,128)} %bitcast.14), calls=%async_computation | async-start | bytes 32768 | tf_op jit(solution)/shard_map/all_to_all | solution.py:71
  61.1 144.3 %all-to-all-start.1 = ((bf16[16,256,400]{1,2,0:T(8,128)(2,1)}), bf16[16,256,400]{1,2,0:T(8,128)(2,1)}, u32[]{:S(2)}, u32[]{:S(2)}) async-start(bf16[16,256,400]{1,2,0:T(8,128)(2,1)} %copy.80), calls=%async_computation.1 | async-start | bytes 6553600 | tf_op jit(solution)/shard_map/all_to_all | solution.py:64
  81.0 100.2 %copy-start.31 = (pred[1000]{0:T(1024)(128)(4,1)}, pred[1000]{0:T(1024)(128)(4,1)S(1)}, u32[]{:S(2)}) copy-start(pred[1000]{0:T(1024)(128)(4,1)S(1)} %and_reduce_fusion) | copy-start | bytes 3004
  81.1 100.2 %copy-start.39 = (pred[1000]{0:T(1024)(128)(4,1)}, pred[1000]{0:T(1024)(128)(4,1)S(1)}, u32[]{:S(2)}) copy-start(pred[1000]{0:T(1024)(128)(4,1)S(1)} %compare_and_fusion.5) | copy-start | bytes 3004
  239.1 32.1 %all-to-all-start.2 = ((bf16[16,256,400]{1,2,0:T(8,128)(2,1)}), bf16[16,256,400]{1,2,0:T(8,128)(2,1)}, u32[]{:S(2)}, u32[]{:S(2)}) async-start(bf16[16,256,400]{1,2,0:T(8,128)(2,1)} %bitcast.130), calls=%async_computation.2 | async-start | bytes 6553600 | tf_op jit(solution)/shard_map/all_to_all | solution.py:98
  243.7 93.5 %all-gather.11.cloned.1.call-start = ((), (), s32[]{:S(2)}) async-start(), calls=%async_computation.7 | async-start | bytes 2359296 | tf_op jit(solution)/shard_map/all_gather | solution.py:23
  296.2 130.4 %all-gather.13.cloned.1.call-start = ((), (), s32[]{:S(2)}) async-start(), calls=%async_computation.8 | async-start | bytes 2359296 | tf_op jit(solution)/shard_map/all_gather | solution.py:23
  302.3 22.6 %collective-permute-start = (f32[1000,400]{0,1:T(8,128)S(1)}, f32[1000,400]{0,1:T(8,128)S(1)}, u32[]{:S(2)}, u32[]{:S(2)}) collective-permute-start(f32[1000,400]{0,1:T(8,128)S(1)} %fusion.79), channel_id=1, source_target_pairs={{0,1},{1,0},{2,3},{3,2},{4,5},{5,4},{6,7},{7,6},{8,9},{9,8},{10,11... | collective-permute-start | bytes 4800008 | tf_op jit(solution)/shard_map/ppermute | solution.py:117
  326.3 42.4 %collective-permute-start.1 = (f32[1000,400]{0,1:T(8,128)}, f32[1000,400]{0,1:T(8,128)}, u32[]{:S(2)}, u32[]{:S(2)}) collective-permute-start(f32[1000,400]{0,1:T(8,128)} %add.270), channel_id=1, source_target_pairs={{0,2},{1,3},{2,0},{3,1},{4,6},{5,7},{6,4},{7,5},{8,10},{9,11},{10,... | collective-permute-start | bytes 4800008 | tf_op jit(solution)/shard_map/ppermute | solution.py:117
  346.8 28.0 %all-to-all-start.3 = ((s32[16,1,256]{2,1,0:T(1,128)}), s32[16,1,256]{2,1,0:T(1,128)S(1)}, u32[]{:S(2)}, u32[]{:S(2)}) async-start(s32[16,1,256]{2,1,0:T(1,128)} %bitcast.32), calls=%async_computation.3 | async-start | bytes 32768 | tf_op jit(solution)/shard_map/all_to_all | solution.py:71
  372.2 25.2 %collective-permute-start.2 = (f32[1000,400]{0,1:T(8,128)}, f32[1000,400]{0,1:T(8,128)}, u32[]{:S(2)}, u32[]{:S(2)}) collective-permute-start(f32[1000,400]{0,1:T(8,128)} %add.271), channel_id=1, source_target_pairs={{0,4},{1,5},{2,6},{3,7},{4,0},{5,1},{6,2},{7,3},{8,12},{9,13},{10,... | collective-permute-start | bytes 4800008 | tf_op jit(solution)/shard_map/ppermute | solution.py:117
  376.7 53.3 %copy-start.43 = (pred[1024]{0:T(1024)(128)(4,1)S(1)}, pred[1024]{0:T(1024)(128)(4,1)}, u32[]{:S(2)}) copy-start(pred[1024]{0:T(1024)(128)(4,1)} %compare_and_fusion.3) | copy-start | bytes 3076
  400.8 97.7 %collective-permute-start.3 = (f32[1000,400]{0,1:T(8,128)}, f32[1000,400]{0,1:T(8,128)}, u32[]{:S(2)}, u32[]{:S(2)}) collective-permute-start(f32[1000,400]{0,1:T(8,128)} %add.272), channel_id=1, source_target_pairs={{0,8},{1,9},{2,10},{3,11},{4,12},{5,13},{6,14},{7,15},{8,0},{9,1},... | collective-permute-start | bytes 4800008 | tf_op jit(solution)/shard_map/ppermute | solution.py:117
  451.7 175.0 %all-to-all-start.4 = ((bf16[16,256,400]{1,2,0:T(8,128)(2,1)}), bf16[16,256,400]{1,2,0:T(8,128)(2,1)}, u32[]{:S(2)}, u32[]{:S(2)}) async-start(bf16[16,256,400]{1,2,0:T(8,128)(2,1)} %copy.90), calls=%async_computation.4 | async-start | bytes 6553600 | tf_op jit(solution)/shard_map/all_to_all | solution.py:64
  660.4 107.1 %all-to-all-start.5 = ((bf16[16,256,400]{1,2,0:T(8,128)(2,1)}), bf16[16,256,400]{1,2,0:T(8,128)(2,1)}, u32[]{:S(2)}, u32[]{:S(2)}) async-start(bf16[16,256,400]{1,2,0:T(8,128)(2,1)} %bitcast.129), calls=%async_computation.5 | async-start | bytes 6553600 | tf_op jit(solution)/shard_map/all_to_all | solution.py:98
  664.9 229.1 %all-gather.15.cloned.1.call-start = ((), (), s32[]{:S(2)}) async-start(), calls=%async_computation.9 | async-start | bytes 2359296 | tf_op jit(solution)/shard_map/all_gather | solution.py:23
  670.9 62.6 %copy-start.18 = (s32[1,1024,1]{1,2,0:T(1,128)S(1)}, s32[1,1024,1]{1,2,0:T(1,128)}, u32[]{:S(2)}) copy-start(s32[1,1024,1]{1,2,0:T(1,128)} %copy-done.17) | copy-start | bytes 12292
  670.9 62.6 %copy-start.23 = (s32[1024]{0:T(1024)S(1)}, s32[1024]{0:T(1024)}, u32[]{:S(2)}) copy-start(s32[1024]{0:T(1024)} %copy-done.22) | copy-start | bytes 12292
  671.0 63.7 %copy-start.45 = (f32[128]{0:T(128)S(1)}, f32[128]{0:T(128)}, u32[]{:S(2)}) copy-start(f32[128]{0:T(128)} %get-tuple-element.37) | copy-start | bytes 1540
  671.0 60.0 %collective-permute-start.4 = (f32[1000,400]{0,1:T(8,128)S(1)}, f32[1000,400]{0,1:T(8,128)S(1)}, u32[]{:S(2)}, u32[]{:S(2)}) collective-permute-start(f32[1000,400]{0,1:T(8,128)S(1)} %fusion.80), channel_id=1, source_target_pairs={{0,1},{1,0},{2,3},{3,2},{4,5},{5,4},{6,7},{7,6},{8,9},{9,8},{10,11... | collective-permute-start | bytes 4800008 | tf_op jit(solution)/shard_map/ppermute | solution.py:117
  732.4 58.4 %collective-permute-start.5 = (f32[1000,400]{0,1:T(8,128)}, f32[1000,400]{0,1:T(8,128)}, u32[]{:S(2)}, u32[]{:S(2)}) collective-permute-start(f32[1000,400]{0,1:T(8,128)} %add.280), channel_id=1, source_target_pairs={{0,2},{1,3},{2,0},{3,1},{4,6},{5,7},{6,4},{7,5},{8,10},{9,11},{10,... | collective-permute-start | bytes 4800008 | tf_op jit(solution)/shard_map/ppermute | solution.py:117
  794.3 37.5 %collective-permute-start.6 = (f32[1000,400]{0,1:T(8,128)}, f32[1000,400]{0,1:T(8,128)}, u32[]{:S(2)}, u32[]{:S(2)}) collective-permute-start(f32[1000,400]{0,1:T(8,128)} %add.281), channel_id=1, source_target_pairs={{0,4},{1,5},{2,6},{3,7},{4,0},{5,1},{6,2},{7,3},{8,12},{9,13},{10,... | collective-permute-start | bytes 4800008 | tf_op jit(solution)/shard_map/ppermute | solution.py:117
  835.3 62.1 %collective-permute-start.7 = (f32[1000,400]{0,1:T(8,128)}, f32[1000,400]{0,1:T(8,128)}, u32[]{:S(2)}, u32[]{:S(2)}) collective-permute-start(f32[1000,400]{0,1:T(8,128)} %add.282), channel_id=1, source_target_pairs={{0,8},{1,9},{2,10},{3,11},{4,12},{5,13},{6,14},{7,15},{8,0},{9,1},... | collective-permute-start | bytes 4800008 | tf_op jit(solution)/shard_map/ppermute | solution.py:117
  (49 other events, 769.0 us)
Sparse Core Ops, SparseCore 0:
  10.3 29.0 all-gather.8
  296.4 40.6 all-gather.10
  341.9 45.6 all-gather.12
  795.3 25.5 all-gather.14
